TPU v7x, 32 devices: a whole 2x2x4 slice. The times are simulated.
32 devices in a mesh: seq: 4 (over y, x), dp: 8 (over z, core).
Axes of the slice: x: 2, y: 2, z: 4, core: 2. Of those that a mesh axis runs over, the one named last changes fastest.
Arguments:
- tokens: bfloat16 [16, 1024, 768], P('dp', 'seq'), may hold values from -6 to 6
- lengths: int32 [16], P('dp'), may hold values from 512 to 1024, as said below
- random_features: float32 [64, 256], replicated, may hold values from -6 to 6
- w_query: bfloat16 [768, 768], P(None, 'dp'), may hold values from -0.21875 to 0.21875
- w_key: bfloat16 [768, 768], P(None, 'dp'), may hold values from -0.21875 to 0.21875
- w_value: bfloat16 [768, 768], P(None, 'dp'), may hold values from -0.21875 to 0.21875
- w_output: bfloat16 [768, 768], P(None, 'dp'), may hold values from -3.5 to 3.5
- w_in: bfloat16 [768, 3072], P(None, 'dp'), may hold values from -0.21875 to 0.21875
- w_out: bfloat16 [3072, 768], P(None, 'dp'), may hold values from -0.109375 to 0.109375
- ln1_gain: bfloat16 [768], P('dp'), may hold values from 0.099609375 to 1.8984375
- ln1_bias: bfloat16 [768], P('dp'), may hold values from -3 to 3
- ln2_gain: bfloat16 [768], P('dp'), may hold values from 0.099609375 to 1.8984375
- ln2_bias: bfloat16 [768], P('dp'), may hold values from -3 to 3
- cotangent: bfloat16 [16, 1024, 768], P('dp', 'seq'), may hold values from -6 to 6
Outputs:
- layer_out: bfloat16 [16, 1024, 768], P('dp', 'seq')
- tokens_grad: float32 [16, 1024, 768], P('dp', 'seq')
- w_query_grad: float32 [768, 768], P(None, 'dp')
- w_key_grad: float32 [768, 768], P(None, 'dp')
- w_value_grad: float32 [768, 768], P(None, 'dp')
- w_output_grad: float32 [768, 768], P(None, 'dp')
- w_in_grad: float32 [768, 3072], P(None, 'dp')
- w_out_grad: float32 [3072, 768], P(None, 'dp')
- ln1_gain_grad: float32 [768], P('dp')
- ln1_bias_grad: float32 [768], P('dp')
- ln2_gain_grad: float32 [768], P('dp')
- ln2_bias_grad: float32 [768], P('dp')
Inputs may be any that keep to these rules, and one draw needn't show every extreme that they name: `lengths`: every sequence holds between 512 and 1024 valid tokens at its start; both ends occur.
All inputs are finite; a program needn't handle non-finite values.
Results may differ from a plain program's by a relative error of at most 0.015.
The roundings to bfloat16 on the way count: a program that leaves them out, or rounds other values in their place, can miss the bound.
Values may be sent and summed in bfloat16 or wider, within the bound.
A program may use at most 192 MiB of HBM per device.

v0:
```python
from functools import partial
import jax
import jax.numpy as jnp
from jax import lax
from jax.sharding import PartitionSpec as P

HEAD = 64
highest = lax.Precision.HIGHEST
norm_epsilon = 1e-12


def layer_norm(row_block, gain_vec, bias_vec):
    mean_val = jnp.mean(row_block, -1, keepdims=True)
    centered = row_block - mean_val
    inv_std = lax.rsqrt(jnp.mean(centered * centered, -1, keepdims=True) + norm_epsilon)
    normed = centered * inv_std
    return (normed * gain_vec + bias_vec, normed, inv_std)


def norm_back(grad_out, normed, inv_std, gain_vec):
    grad_normed = grad_out * gain_vec
    inner_term = (
        grad_normed
        - jnp.mean(grad_normed, -1, keepdims=True)
        - normed * jnp.mean(grad_normed * normed, -1, keepdims=True)
    )
    return (inv_std * inner_term, jnp.sum(grad_out * normed, 0), jnp.sum(grad_out, 0))


def row_product(left, right):
    return lax.dot_general(
        left, right, (((0,), (0,)), ((), ())), preferred_element_type=jnp.float32
    )


def feature_map(projected, random_features):
    scaled = projected.astype(jnp.float32) * HEAD ** (-0.25)
    projection = jnp.einsum("snhe,em->snhm", scaled, random_features, precision=highest)
    return (jnp.exp(projection - 0.5 * jnp.sum(scaled * scaled, -1, keepdims=True)), scaled)


def feature_back(grad_features, features, scaled, random_features):
    grad_proj = grad_features * features
    grad_scaled = jnp.einsum("snhm,em->snhe", grad_proj, random_features, precision=highest)
    grad_scaled = grad_scaled - scaled * jnp.sum(grad_proj, -1, keepdims=True)
    return grad_scaled * HEAD ** (-0.25)


def keep_local(key_state, key_total):
    return (key_state, key_total)


def mixer_forward(queries, key_proj, value_proj, key_mask, random_features, reducer):
    q_feat, q_scaled = feature_map(queries, random_features)
    k_feat, k_scaled = feature_map(key_proj, random_features)
    k_feat = k_feat * key_mask[:, :, None, None]
    key_state = jnp.einsum(
        "snhm,snhe->shme", k_feat, value_proj.astype(jnp.float32), precision=highest
    )
    key_total = jnp.sum(k_feat, 1)
    key_state, key_total = reducer(key_state, key_total)
    numerator = jnp.einsum("snhm,shme->snhe", q_feat, key_state, precision=highest)
    denominator = jnp.einsum("snhm,shm->snh", q_feat, key_total, precision=highest)
    context = numerator / denominator[..., None]
    return (
        context,
        (q_feat, q_scaled, k_feat, k_scaled, key_state, key_total, denominator, context),
    )


def mixer_backward(grad_context, value_proj, kept_mixer, random_features, reducer):
    q_feat, q_scaled, k_feat, k_scaled, key_state, key_total, denominator, context = kept_mixer
    grad_ctx = grad_context.astype(jnp.float32)
    grad_num = grad_ctx / denominator[..., None]
    grad_den = -jnp.sum(grad_ctx * context, -1) / denominator
    grad_qfeat = (
        jnp.einsum("snhe,shme->snhm", grad_num, key_state, precision=highest)
        + grad_den[..., None] * key_total[:, None]
    )
    grad_state = jnp.einsum("snhm,snhe->shme", q_feat, grad_num, precision=highest)
    grad_total = jnp.einsum("snhm,snh->shm", q_feat, grad_den, precision=highest)
    grad_state, grad_total = reducer(grad_state, grad_total)
    values_f32 = value_proj.astype(jnp.float32)
    grad_kfeat = (
        jnp.einsum("snhe,shme->snhm", values_f32, grad_state, precision=highest)
        + grad_total[:, None]
    )
    grad_values = jnp.einsum("snhm,shme->snhe", k_feat, grad_state, precision=highest)
    grad_queries = feature_back(grad_qfeat, q_feat, q_scaled, random_features)
    grad_keys = feature_back(grad_kfeat, k_feat, k_scaled, random_features)
    return (grad_queries, grad_keys, grad_values)


def shards(
    tokens,
    lengths,
    random_features,
    w_query,
    w_key,
    w_value,
    w_output,
    w_in,
    w_out,
    ln1_gain,
    ln1_bias,
    ln2_gain,
    ln2_bias,
    cotangent,
):
    seq_count, local_len, model_width = tokens.shape
    row_count = seq_count * local_len
    seq_parts = lax.axis_size("seq")
    heads_all = model_width // HEAD
    wq_full, wk_full, wv_full, wo_full, win_full, wout_full, gain1, bias1, gain2, bias2 = (
        lax.all_gather(w_query, "dp", axis=1, tiled=True),
        lax.all_gather(w_key, "dp", axis=1, tiled=True),
        lax.all_gather(w_value, "dp", axis=1, tiled=True),
        lax.all_gather(w_output, "dp", axis=1, tiled=True),
        lax.all_gather(w_in, "dp", axis=1, tiled=True),
        lax.all_gather(w_out, "dp", axis=1, tiled=True),
        lax.all_gather(ln1_gain, "dp", axis=0, tiled=True),
        lax.all_gather(ln1_bias, "dp", axis=0, tiled=True),
        lax.all_gather(ln2_gain, "dp", axis=0, tiled=True),
        lax.all_gather(ln2_bias, "dp", axis=0, tiled=True),
    )
    tok_rows = tokens.reshape(row_count, model_width)
    query_proj = jnp.dot(tok_rows, wq_full, preferred_element_type=jnp.float32).astype(jnp.bfloat16)
    key_proj = jnp.dot(tok_rows, wk_full, preferred_element_type=jnp.float32).astype(jnp.bfloat16)
    value_proj = jnp.dot(tok_rows, wv_full, preferred_element_type=jnp.float32).astype(jnp.bfloat16)
    local_pos = lax.axis_index("seq") * local_len + jnp.arange(local_len, dtype=jnp.int32)
    row_valid = (local_pos[None, :] < lengths[:, None]).astype(jnp.float32)
    full_len = local_len * seq_parts
    head_group = heads_all // seq_parts
    q_heads, k_heads, v_heads = (
        lax.all_to_all(
            query_proj.reshape(seq_count, local_len, model_width),
            "seq",
            split_axis=2,
            concat_axis=1,
            tiled=True,
        ),
        lax.all_to_all(
            key_proj.reshape(seq_count, local_len, model_width),
            "seq",
            split_axis=2,
            concat_axis=1,
            tiled=True,
        ),
        lax.all_to_all(
            value_proj.reshape(seq_count, local_len, model_width),
            "seq",
            split_axis=2,
            concat_axis=1,
            tiled=True,
        ),
    )
    q_heads = q_heads.reshape(seq_count, full_len, head_group, HEAD)
    k_heads = k_heads.reshape(seq_count, full_len, head_group, HEAD)
    v_heads = v_heads.reshape(seq_count, full_len, head_group, HEAD)
    full_pos = jnp.arange(full_len, dtype=jnp.int32)
    key_mask = (full_pos[None, :] < lengths[:, None]).astype(jnp.float32)
    context, kept_mixer = mixer_forward(
        q_heads, k_heads, v_heads, key_mask, random_features, keep_local
    )
    ctx_low = context.astype(jnp.bfloat16).reshape(seq_count, full_len, head_group * HEAD)
    ctx_tokens = lax.all_to_all(ctx_low, "seq", split_axis=1, concat_axis=2, tiled=True)
    ctx_rows = ctx_tokens.reshape(row_count, model_width)
    attn_out = jnp.dot(ctx_rows, wo_full, preferred_element_type=jnp.float32)
    resid1 = tok_rows.astype(jnp.float32) + attn_out
    hidden, normed1, inv1 = layer_norm(resid1, gain1.astype(jnp.float32), bias1.astype(jnp.float32))
    hidden_low = hidden.astype(jnp.bfloat16)
    pre_act = jnp.dot(hidden_low, win_full, preferred_element_type=jnp.float32)
    activated, gelu_pull = jax.vjp(partial(jax.nn.gelu, approximate=False), pre_act)
    act_low = activated.astype(jnp.bfloat16)
    ffn_out = jnp.dot(act_low, wout_full, preferred_element_type=jnp.float32)
    normed_out, normed2, inv2 = layer_norm(
        hidden + ffn_out, gain2.astype(jnp.float32), bias2.astype(jnp.float32)
    )
    valid_rows = row_valid.reshape(row_count, 1)
    layer_out = (
        (normed_out * valid_rows).astype(jnp.bfloat16).reshape(seq_count, local_len, model_width)
    )
    wq_back, wk_back, wv_back, wo_back, win_back, wout_back, gain1_back, gain2_back = (
        lax.all_gather(w_query, "dp", axis=1, tiled=True),
        lax.all_gather(w_key, "dp", axis=1, tiled=True),
        lax.all_gather(w_value, "dp", axis=1, tiled=True),
        lax.all_gather(w_output, "dp", axis=1, tiled=True),
        lax.all_gather(w_in, "dp", axis=1, tiled=True),
        lax.all_gather(w_out, "dp", axis=1, tiled=True),
        lax.all_gather(ln1_gain, "dp", axis=0, tiled=True),
        lax.all_gather(ln2_gain, "dp", axis=0, tiled=True),
    )
    grad_y = cotangent.reshape(row_count, model_width).astype(jnp.float32) * valid_rows
    grad_r2, grad_gain2, grad_bias2 = norm_back(
        grad_y, normed2, inv2, gain2_back.astype(jnp.float32)
    )
    grad_ffn = grad_r2.astype(jnp.bfloat16)
    grad_wout = row_product(act_low, grad_ffn)
    grad_act = lax.dot_general(
        grad_ffn, wout_back, (((1,), (1,)), ((), ())), preferred_element_type=jnp.float32
    )
    grad_pre = gelu_pull(grad_act)[0].astype(jnp.bfloat16)
    grad_win = row_product(hidden_low, grad_pre)
    grad_hidden = grad_r2 + lax.dot_general(
        grad_pre, win_back, (((1,), (1,)), ((), ())), preferred_element_type=jnp.float32
    )
    grad_r1, grad_gain1, grad_bias1 = norm_back(
        grad_hidden, normed1, inv1, gain1_back.astype(jnp.float32)
    )
    grad_attn = grad_r1.astype(jnp.bfloat16)
    grad_wo = row_product(ctx_rows, grad_attn)
    grad_ctx = lax.dot_general(
        grad_attn, wo_back, (((1,), (1,)), ((), ())), preferred_element_type=jnp.float32
    ).astype(jnp.bfloat16)
    grad_heads = lax.all_to_all(
        grad_ctx.reshape(seq_count, local_len, model_width),
        "seq",
        split_axis=2,
        concat_axis=1,
        tiled=True,
    )
    grad_heads = grad_heads.reshape(seq_count, full_len, head_group, HEAD)
    grad_q, grad_k, grad_v = mixer_backward(
        grad_heads, v_heads, kept_mixer, random_features, keep_local
    )
    grad_q_tok, grad_k_tok, grad_v_tok = (
        lax.all_to_all(
            grad_q.astype(jnp.bfloat16).reshape(seq_count, full_len, head_group * HEAD),
            "seq",
            split_axis=1,
            concat_axis=2,
            tiled=True,
        ),
        lax.all_to_all(
            grad_k.astype(jnp.bfloat16).reshape(seq_count, full_len, head_group * HEAD),
            "seq",
            split_axis=1,
            concat_axis=2,
            tiled=True,
        ),
        lax.all_to_all(
            grad_v.astype(jnp.bfloat16).reshape(seq_count, full_len, head_group * HEAD),
            "seq",
            split_axis=1,
            concat_axis=2,
            tiled=True,
        ),
    )
    grad_q_rows = grad_q_tok.reshape(row_count, model_width)
    grad_k_rows = grad_k_tok.reshape(row_count, model_width)
    grad_v_rows = grad_v_tok.reshape(row_count, model_width)
    grad_wq = row_product(tok_rows, grad_q_rows)
    grad_wk = row_product(tok_rows, grad_k_rows)
    grad_wv = row_product(tok_rows, grad_v_rows)
    contract_out = (((1,), (1,)), ((), ()))
    grad_tokens = grad_r1 + lax.dot_general(
        grad_q_rows, wq_back, contract_out, preferred_element_type=jnp.float32
    )
    grad_tokens = grad_tokens + lax.dot_general(
        grad_k_rows, wk_back, contract_out, preferred_element_type=jnp.float32
    )
    grad_tokens = grad_tokens + lax.dot_general(
        grad_v_rows, wv_back, contract_out, preferred_element_type=jnp.float32
    )
    (
        share_wq,
        share_wk,
        share_wv,
        share_wo,
        share_win,
        share_wout,
        share_g1,
        share_b1,
        share_g2,
        share_b2,
    ) = (
        lax.psum_scatter(grad_wq, "dp", scatter_dimension=1, tiled=True),
        lax.psum_scatter(grad_wk, "dp", scatter_dimension=1, tiled=True),
        lax.psum_scatter(grad_wv, "dp", scatter_dimension=1, tiled=True),
        lax.psum_scatter(grad_wo, "dp", scatter_dimension=1, tiled=True),
        lax.psum_scatter(grad_win, "dp", scatter_dimension=1, tiled=True),
        lax.psum_scatter(grad_wout, "dp", scatter_dimension=1, tiled=True),
        lax.psum_scatter(grad_gain1, "dp", scatter_dimension=0, tiled=True),
        lax.psum_scatter(grad_bias1, "dp", scatter_dimension=0, tiled=True),
        lax.psum_scatter(grad_gain2, "dp", scatter_dimension=0, tiled=True),
        lax.psum_scatter(grad_bias2, "dp", scatter_dimension=0, tiled=True),
    )
    (
        final_wq,
        final_wk,
        final_wv,
        final_wo,
        final_win,
        final_wout,
        final_g1,
        final_b1,
        final_g2,
        final_b2,
    ) = (
        lax.psum(share_wq.astype(jnp.bfloat16), "seq").astype(jnp.float32),
        lax.psum(share_wk.astype(jnp.bfloat16), "seq").astype(jnp.float32),
        lax.psum(share_wv.astype(jnp.bfloat16), "seq").astype(jnp.float32),
        lax.psum(share_wo.astype(jnp.bfloat16), "seq").astype(jnp.float32),
        lax.psum(share_win.astype(jnp.bfloat16), "seq").astype(jnp.float32),
        lax.psum(share_wout.astype(jnp.bfloat16), "seq").astype(jnp.float32),
        lax.psum(share_g1.astype(jnp.bfloat16), "seq").astype(jnp.float32),
        lax.psum(share_b1.astype(jnp.bfloat16), "seq").astype(jnp.float32),
        lax.psum(share_g2.astype(jnp.bfloat16), "seq").astype(jnp.float32),
        lax.psum(share_b2.astype(jnp.bfloat16), "seq").astype(jnp.float32),
    )
    return (
        layer_out,
        grad_tokens.reshape(seq_count, local_len, model_width),
        final_wq,
        final_wk,
        final_wv,
        final_wo,
        final_win,
        final_wout,
        final_g1,
        final_b1,
        final_g2,
        final_b2,
    )


def solution(mesh):
    in_specs = (
        P("dp", "seq", None),
        P("dp"),
        P(),
        P(None, "dp"),
        P(None, "dp"),
        P(None, "dp"),
        P(None, "dp"),
        P(None, "dp"),
        P(None, "dp"),
        P("dp"),
        P("dp"),
        P("dp"),
        P("dp"),
        P("dp", "seq", None),
    )
    out_specs = (
        P("dp", "seq", None),
        P("dp", "seq", None),
        P(None, "dp"),
        P(None, "dp"),
        P(None, "dp"),
        P(None, "dp"),
        P(None, "dp"),
        P(None, "dp"),
        P("dp"),
        P("dp"),
        P("dp"),
        P("dp"),
    )
    return jax.shard_map(shards, mesh=mesh, in_specs=in_specs, out_specs=out_specs, check_vma=False)
```

profile of v0, /device:TPU:0, one launch (start us, length us, event | category | flops | bytes accessed | tf_op | source)
XLA Modules:
  0.0 704.7 jit_solution(9426483692324572481)
XLA Ops:
  10.6 24.6 %all-gather.7.cloned.1.call-done = bf16[768,768]{0,1:T(8,128)(2,1)} async-done(((bf16[768,96]{0,1:T(8,128)(2,1)}), bf16[768,768]{0,1:T(8,128)(2,1)}) %all-gather.7.cloned.1.call-update) | async-done | bytes 1179664 | tf_op jit(solution)/shard_map/all_gather | solution.py:116
  35.2 2.3 convolution_convert_fusion.3
  39.3 3.5 all-to-all-start
  43.5 15.9 %all-gather.11.cloned.1.call-done = bf16[768,768]{0,1:T(8,128)(2,1)} async-done(((bf16[768,96]{0,1:T(8,128)(2,1)}), bf16[768,768]{0,1:T(8,128)(2,1)}) %all-gather.11.cloned.1.call-update) | async-done | bytes 1179664 | tf_op jit(solution)/shard_map/all_gather | solution.py:115
  63.3 4.2 all-to-all-start.2
  69.8 16.1 %all-reduce.9 = (bf16[768]{0:T(1024)(128)(2,1)S(1)}, bf16[768]{0:T(1024)(128)(2,1)S(1)}, bf16[768]{0:T(1024)(128)(2,1)S(1)}, bf16[768]{0:T(1024)(128)(2,1)S(1)}) all-reduce(bf16[768]{0:T(1024)(128)(2,1)S(1)} %dynamic-update-slice.1, bf16[768]{0:T(1024)(128)(2,1)S(1)} %dynamic-update-slice, ...), channel_id=1, replica_groups=mesh['seq'=4,'dp'=8] {'dp'}, use_global_device_ids=true, to_apply=%add.1 | all-reduce | flops 3072 | bytes 12288
  91.9 4.4 all-to-all-start.1
  102.4 3.3 all-to-all-done.1
  108.5 2.5 reshape.223
  111.0 7.3 %fusion.20 = f32[2,1024,3,256]{1,3,2,0:T(8,128)S(1)} fusion(f32[2,1024,3,64]{1,3,2,0:T(8,128)S(1)} %reshape.237, f32[64,256]{1,0:T(8,128)S(1)} %copy-done), kind=kOutput, calls=%fused_computation.64 | convolution fusion | flops 1208352768 | bytes 7929856 | tf_op jit(solution)/shard_map/snhe,em->snhm/dot_general | solution.py:38
  118.4 7.2 %fusion.16 = (f32[2,3,256]{2,1,0:T(4,128)S(1)}, f32[2,1024,3,256]{3,1,2,0:T(8,128)S(1)}) fusion(f32[2,1024]{1,0:T(2,128)S(1)} %compare_convert_fusion, f32[2,1024,3]{1,2,0:T(4,128)S(1)} %broadcast_multiply_fusion.3, f32[64,256]{1,0:T(8,128)S(1)} %copy-done, f32[2,1024,3,64]{1,3,2,0:T(8,128)S(1)} %reshape.236), kind=kOutput, calls=%fused_computation.31 | convolution fusion | flops 1213069824 | bytes 7968768 | tf_op jit(solution)/shard_map/snhe,em->snhm/dot_general | solution.py:38
  125.6 3.6 fusion.9
  129.3 3.6 fusion.17
  132.9 5.6 fusion.52
  140.4 3.5 all-to-all-start.3
  144.6 12.6 %all-to-all-done.3 = bf16[2,1024,192]{2,0,1:T(2,128)(2,1)S(1)} async-done(((bf16[2,1024,192]{2,0,1:T(2,128)(2,1)}), bf16[2,1024,192]{2,0,1:T(2,128)(2,1)S(1)}, u32[]{:S(2)}, u32[]{:S(2)}) %all-to-all-start.3) | async-done | bytes 786464 | tf_op jit(solution)/shard_map/all_to_all | solution.py:166
  158.1 4.2 copy.97
  165.3 2.5 fusion.53
  169.2 20.7 %multiply_convert_fusion = (bf16[512,3072]{1,0:T(8,128)(2,1)}, f32[512,3072]{1,0:T(8,128)}, f32[512,3072]{1,0:T(8,128)}) fusion(bf16[768,3072]{1,0:T(8,128)(2,1)} %all-gather.15.cloned.1.call-done, f32[512,768]{1,0:T(8,128)} %copy-done.21, f32[768]{0:T(1024)S(1)} %convert_element_type.205, f32[768]{0:T(1024)S(1)} %convert_element_type.204, ...), kind=kOutput, calls=%fused_computation.6 | convolution fusion | flops 2520121344 | bytes 22030336 | tf_op jit(solution)/shard_map/dot_general | solution.py:172
  190.0 21.4 %all-gather.17.cloned.1.call-done = bf16[3072,768]{0,1:T(8,128)(2,1)} async-done(((bf16[3072,96]{0,1:T(8,128)(2,1)}), bf16[3072,768]{0,1:T(8,128)(2,1)}) %all-gather.17.cloned.1.call-update) | async-done | bytes 4718608 | tf_op jit(solution)/shard_map/all_gather | solution.py:120
  211.4 6.6 fusion.54
  220.7 7.7 %add_convert_fusion = bf16[512,3072]{1,0:T(8,128)(2,1)S(1)} fusion(f32[512,3072]{1,0:T(8,128)S(1)} %copy-done.41, f32[512,3072]{1,0:T(8,128)} %get-tuple-element.52, bf16[3072,768]{0,1:T(8,128)(2,1)S(1)} %copy-done.33, f32[512,768]{1,0:T(8,128)S(1)} %get-tuple-element.40), kind=kOutput, calls=%fused_computation.5 | convolution fusion | flops 2438332416 | bytes 22020096 | tf_op jit(solution)/shard_map/dot_general | solution.py:199
  228.5 3.1 multiply_reduce_fusion.1
  235.0 2.9 convolution_convert_fusion
  237.9 2.3 copy.73
  240.3 15.4 %all_to_all.102 = bf16[2,256,768]{1,0,2:T(2,128)(2,1)S(1)} all-to-all(bf16[2,256,768]{1,0,2:T(2,128)(2,1)S(1)} %copy.73), channel_id=1, replica_groups=mesh['seq'=4,'dp'=8] {'seq'}, dimensions={2} | all-to-all | bytes 1572864 | tf_op jit(solution)/shard_map/all_to_all | solution.py:215
  258.0 3.1 reshape.240
  261.1 10.2 %fusion.8 = f32[2,3,256,64]{2,3,1,0:T(8,128)S(1)} fusion(f32[2,1024,3,256]{1,3,2,0:T(8,128)} %copy-done.1, f32[2,1024,3]{1,2,0:T(4,128)S(1)} %broadcast_multiply_fusion.2, f32[2,1024,3,64]{1,3,2,0:T(8,128)} %reshape.240, f32[2,1024,3]{1,2,0:T(4,128)S(1)} %bitcast.205), kind=kOutput, calls=%fused_computation.23 | convolution fusion | flops 1209925632 | bytes 8306688 | tf_op jit(solution)/shard_map/snhm,snhe->shme/dot_general | solution.py:80
  271.3 7.8 %fusion.24 = bf16[2,3,64,1024]{3,2,1,0:T(8,128)(2,1)} fusion(f32[2,3,256,64]{2,3,1,0:T(8,128)S(1)} %fusion.8, f32[2,1024,3,256]{3,1,2,0:T(8,128)S(1)} %bitcast.160, f32[2,1024]{1,0:T(2,128)S(1)} %compare_convert_fusion, f32[2,1024,3]{1,2,0:T(4,128)S(1)} %broadcast_multiply_fusion.3), kind=kOutput, calls=%fused_computation.74 | convolution fusion | flops 1211498496 | bytes 7503872 | tf_op jit(solution)/shard_map/snhm,shme->snhe/dot_general | solution.py:88
  279.2 2.5 copy.85
  281.6 15.8 %all_to_all.103 = bf16[2,1024,192]{2,0,1:T(2,128)(2,1)S(1)} all-to-all(bf16[2,1024,192]{2,0,1:T(2,128)(2,1)S(1)} %copy.85), channel_id=1, replica_groups=mesh['seq'=4,'dp'=8] {'seq'}, dimensions={1} | all-to-all | bytes 1572864 | tf_op jit(solution)/shard_map/all_to_all | solution.py:241
  303.6 2.4 multiply_reduce_fusion.2
  306.0 8.4 %fusion.7 = f32[2,3,1,256]{3,2,1,0:T(1,128)S(1)} fusion(f32[2,1024,3,256]{1,3,2,0:T(8,128)} %copy-done.1, f32[2,1024,3]{1,2,0:T(4,128)S(1)} %broadcast_multiply_fusion.2, f32[2,1024,3,1]{1,2,0,3:T(4,128)S(1)} %bitcast.207), kind=kOutput, calls=%fused_computation.22 | convolution fusion | flops 20447232 | bytes 6346752 | tf_op jit(solution)/shard_map/snhm,snh->shm/dot_general | solution.py:81
  314.5 4.8 fusion.55
  319.4 6.2 multiply_convert_fusion.1
  326.5 14.7 %all_to_all.104 = bf16[2,1024,192]{2,0,1:T(2,128)(2,1)S(1)} all-to-all(bf16[2,1024,192]{2,0,1:T(2,128)(2,1)S(1)} %copy.82), channel_id=1, replica_groups=mesh['seq'=4,'dp'=8] {'seq'}, dimensions={1} | all-to-all | bytes 1572864 | tf_op jit(solution)/shard_map/all_to_all | solution.py:234
  345.0 2.3 convolution_bitcast_fusion.1
  347.4 11.6 %fusion.56 = (f32[2,1024,3]{1,2,0:T(4,128)S(1)}, f32[2,1024,3,256]{1,3,2,0:T(8,128)S(1)}) fusion(f32[2,1024,3,256]{1,3,2,0:T(8,128)} %copy-done.1, f32[2,1024,3]{1,2,0:T(4,128)S(1)} %broadcast_multiply_fusion.2, f32[2,3,256]{2,1,0:T(4,128)S(1)} %get-tuple-element.46, f32[2,1024,3]{1,2,0:T(4,128)S(1)} %negate_divide_fusion, ...), kind=kOutput, calls=%fused_computation.125 | convolution fusion | flops 1216210944 | bytes 14653440 | tf_op jit(solution)/shard_map/snhe,shme->snhm/dot_general | solution.py:77
  359.1 4.3 multiply_convert_fusion.2
  364.3 13.4 %all_to_all.105 = bf16[2,1024,192]{2,0,1:T(2,128)(2,1)S(1)} all-to-all(bf16[2,1024,192]{2,0,1:T(2,128)(2,1)S(1)} %copy.77), channel_id=1, replica_groups=mesh['seq'=4,'dp'=8] {'seq'}, dimensions={1} | all-to-all | bytes 1572864 | tf_op jit(solution)/shard_map/all_to_all | solution.py:227
  382.9 7.2 %fusion.46 = f32[768,3072]{1,0:T(8,128)} fusion(bf16[512,3072]{1,0:T(8,128)(2,1)} %copy-done.40, f32[512,768]{1,0:T(8,128)S(1)} %copy-done.23, f32[768]{0:T(1024)S(1)} %convert_element_type.205, f32[768]{0:T(1024)S(1)} %convert_element_type.204, f32[512]{0:T(512)S(1)} %add_rsqrt_fusion.1, f32[512]{0:T(512)S(1)} %broadcast_multiply_fusion.8), kind=kOutput, calls=%fused_computation.118 | convolution fusion | flops 2417885184 | bytes 14166016 | tf_op jit(solution)/shard_map/dot_general | solution.py:31
  391.5 7.0 fusion.31
  403.5 16.4 %reduce-scatter.7.cloned.1.call-done = f32[768,96]{0,1:T(8,128)} async-done(((f32[768,768]{0,1:T(8,128)}), f32[768,96]{0,1:T(8,128)}) %reduce-scatter.7.cloned.1.call-update) | async-done | bytes 294928 | tf_op jit(solution)/shard_map/reduce_scatter | solution.py:277
  421.5 98.9 %reduce-scatter.15.cloned.1.call-done = f32[768,384]{1,0:T(8,128)} async-done(((f32[768,3072]{1,0:T(8,128)}), f32[768,384]{1,0:T(8,128)}) %reduce-scatter.15.cloned.1.call-update) | async-done | bytes 1179664 | tf_op jit(solution)/shard_map/reduce_scatter | solution.py:281
  522.6 97.9 %reduce-scatter.17.cloned.1.call-done = f32[3072,96]{0,1:T(8,128)} async-done(((f32[3072,768]{0,1:T(8,128)}), f32[3072,96]{0,1:T(8,128)}) %reduce-scatter.17.cloned.1.call-update) | async-done | bytes 1179664 | tf_op jit(solution)/shard_map/reduce_scatter | solution.py:282
  623.4 25.9 %all-reduce.8 = (bf16[768]{0:T(1024)(128)(2,1)S(1)}, bf16[768]{0:T(1024)(128)(2,1)S(1)}, bf16[768]{0:T(1024)(128)(2,1)S(1)}, bf16[768]{0:T(1024)(128)(2,1)S(1)}) all-reduce(f32[768]{0:T(1024)S(1)} %get-tuple-element.12, f32[768]{0:T(1024)S(1)} %get-tuple-element.17, ...), channel_id=8, replica_groups=mesh['seq'=4,'dp'=8] {'dp'}, use_global_device_ids=true, to_apply=%region_27.0.clone | all-reduce | flops 3072 | bytes 18432
  649.6 9.9 %all-reduce.10 = (bf16[96]{0:T(256)(128)(2,1)S(1)}, bf16[96]{0:T(256)(128)(2,1)S(1)}, bf16[96]{0:T(256)(128)(2,1)S(1)}, bf16[96]{0:T(256)(128)(2,1)S(1)}) all-reduce(bf16[96]{0:T(256)(128)(2,1)S(1)} %dynamic-slice.19, bf16[96]{0:T(256)(128)(2,1)S(1)} %dynamic-slice.18, ...), channel_id=1, replica_groups=mesh['seq'=4,'dp'=8] {'seq'}, use_global_device_ids=true, to_apply=%region_28.0 | all-reduce | flops 384 | bytes 1536 | tf_op jit(solution)/shard_map/psum | solution.py:306
  667.3 20.8 %all-reduce.14.cloned.1.call-done = (bf16[768,96]{0,1:T(8,128)(2,1)}, bf16[768,96]{0,1:T(8,128)(2,1)}, bf16[768,96]{0,1:T(8,128)(2,1)}, bf16[768,96]{0,1:T(8,128...) async-done(((bf16[768,96]{0,1:T(8,128)(2,1)}, bf16[768,96]{0,1:T(8,128)(2,1)}, bf16[768,96]{0,1:T(8,128)(2,1)}, bf16[768,96]{0,1:T(8,128)(2,1)}, ...) | async-done | bytes 1769488 | tf_op jit(solution)/shard_map/psum | solution.py:300
  (231 shorter events, 89.7 us)
Async XLA Ops:
  7.2 103.8 %copy-start = (f32[64,256]{1,0:T(8,128)S(1)}, f32[64,256]{1,0:T(8,128)}, u32[]{:S(2)}) copy-start(f32[64,256]{1,0:T(8,128)} %param.16) | copy-start | bytes 196612
  7.2 28.0 %all-gather.7.cloned.1.call-start = ((), (), s32[]{:S(2)}) async-start(), calls=%async_computation.14 | async-start | bytes 1327104 | tf_op jit(solution)/shard_map/all_gather | solution.py:116
  7.9 51.4 %all-gather.11.cloned.1.call-start = ((), (), s32[]{:S(2)}) async-start(), calls=%async_computation.16 | async-start | bytes 1327104 | tf_op jit(solution)/shard_map/all_gather | solution.py:115
  8.7 77.2 %all-gather.9.cloned.1.call-start = ((), (), s32[]{:S(2)}) async-start(), calls=%async_computation.15 | async-start | bytes 1327104 | tf_op jit(solution)/shard_map/all_gather | solution.py:117
  9.4 155.9 %all-gather.13.cloned.1.call-start = ((), (), s32[]{:S(2)}) async-start(), calls=%async_computation.17 | async-start | bytes 1327104 | tf_op jit(solution)/shard_map/all_gather | solution.py:118
  10.0 159.2 %all-gather.15.cloned.1.call-start = ((), (), s32[]{:S(2)}) async-start(), calls=%async_computation.18 | async-start | bytes 5308416 | tf_op jit(solution)/shard_map/all_gather | solution.py:119
  37.5 5.9 copy-start.32
  37.5 21.9 %copy-start.12 = (bf16[2,256,768]{2,1,0:T(8,128)(2,1)S(1)}, bf16[2,256,768]{2,1,0:T(8,128)(2,1)}, u32[]{:S(2)}) copy-start(bf16[2,256,768]{2,1,0:T(8,128)(2,1)} %param.14) | copy-start | bytes 2359300
  39.3 24.0 %all-to-all-start = ((bf16[2,256,768]{1,0,2:T(2,128)(2,1)}), bf16[2,256,768]{1,0,2:T(2,128)(2,1)S(1)}, u32[]{:S(2)}, u32[]{:S(2)}) async-start(bf16[2,256,768]{1,0,2:T(2,128)(2,1)} %copy.60), calls=%async_computation | async-start | bytes 1572864 | tf_op jit(solution)/shard_map/all_to_all | solution.py:142
  42.9 168.5 %all-gather.17.cloned.1.call-start = ((), (), s32[]{:S(2)}) async-start(), calls=%async_computation.19 | async-start | bytes 5308416 | tf_op jit(solution)/shard_map/all_gather | solution.py:120
  61.5 6.1 copy-start.31
  61.5 7.3 %copy-start.36 = (bf16[96]{0:T(256)(128)(2,1)S(1)}, bf16[96]{0:T(256)(128)(2,1)}, u32[]{:S(2)}) copy-start(bf16[96]{0:T(256)(128)(2,1)} %param.26) | copy-start | bytes 580
  61.5 7.6 %copy-start.37 = (bf16[96]{0:T(256)(128)(2,1)S(1)}, bf16[96]{0:T(256)(128)(2,1)}, u32[]{:S(2)}) copy-start(bf16[96]{0:T(256)(128)(2,1)} %param.23) | copy-start | bytes 580
  61.5 7.8 %copy-start.38 = (bf16[96]{0:T(256)(128)(2,1)S(1)}, bf16[96]{0:T(256)(128)(2,1)}, u32[]{:S(2)}) copy-start(bf16[96]{0:T(256)(128)(2,1)} %param.24) | copy-start | bytes 580
  61.5 8.0 %copy-start.39 = (bf16[96]{0:T(256)(128)(2,1)S(1)}, bf16[96]{0:T(256)(128)(2,1)}, u32[]{:S(2)}) copy-start(bf16[96]{0:T(256)(128)(2,1)} %param.25) | copy-start | bytes 580
  63.3 28.6 %all-to-all-start.2 = ((bf16[2,256,768]{1,0,2:T(2,128)(2,1)}), bf16[2,256,768]{1,0,2:T(2,128)(2,1)}, u32[]{:S(2)}, u32[]{:S(2)}) async-start(bf16[2,256,768]{1,0,2:T(2,128)(2,1)} %copy.66), calls=%async_computation.2 | async-start | bytes 1572864 | tf_op jit(solution)/shard_map/all_to_all | solution.py:135
  91.9 26.5 %copy-start.3 = (f32[2,1024,3,64]{1,3,2,0:T(8,128)}, f32[2,1024,3,64]{1,3,2,0:T(8,128)S(1)}, u32[]{:S(2)}) copy-start(f32[2,1024,3,64]{1,3,2,0:T(8,128)S(1)} %reshape.236) | copy-start | bytes 4718596
  91.9 13.8 %all-to-all-start.1 = ((bf16[2,256,768]{1,0,2:T(2,128)(2,1)}), bf16[2,256,768]{1,0,2:T(2,128)(2,1)}, u32[]{:S(2)}, u32[]{:S(2)}) async-start(bf16[2,256,768]{1,0,2:T(2,128)(2,1)} %copy.63), calls=%async_computation.1 | async-start | bytes 1572864 | tf_op jit(solution)/shard_map/all_to_all | solution.py:149
  101.9 9.1 %copy-start.5 = (f32[2,1024,3,64]{1,3,2,0:T(8,128)}, f32[2,1024,3,64]{1,3,2,0:T(8,128)S(1)}, u32[]{:S(2)}) copy-start(f32[2,1024,3,64]{1,3,2,0:T(8,128)S(1)} %reshape.237) | copy-start | bytes 4718596
  118.4 14.5 %copy-start.1 = (f32[2,1024,3,256]{1,3,2,0:T(8,128)}, f32[2,1024,3,256]{1,3,2,0:T(8,128)S(1)}, u32[]{:S(2)}) copy-start(f32[2,1024,3,256]{1,3,2,0:T(8,128)S(1)} %fusion.20) | copy-start | bytes 18874372
  125.6 3.7 copy-start.2
  125.6 3.7 copy-start.10
  132.8 5.6 copy-start.25
  138.4 5.7 copy-start.11
  140.4 16.7 %all-to-all-start.3 = ((bf16[2,1024,192]{2,0,1:T(2,128)(2,1)}), bf16[2,1024,192]{2,0,1:T(2,128)(2,1)S(1)}, u32[]{:S(2)}, u32[]{:S(2)}) async-start(bf16[2,1024,192]{2,0,1:T(2,128)(2,1)} %copy.70), calls=%async_computation.3 | async-start | bytes 2097152 | tf_op jit(solution)/shard_map/all_to_all | solution.py:166
  144.0 254.6 %reduce-scatter.13.cloned.1.call-start = ((), (), s32[]{:S(2)}) async-start(), calls=%async_computation.23 | async-start | bytes 2654208 | tf_op jit(solution)/shard_map/reduce_scatter | solution.py:280
  158.1 7.2 %copy-start.13 = (bf16[2,256,768]{2,1,0:T(8,128)(2,1)S(1)}, bf16[2,256,768]{2,1,0:T(8,128)(2,1)}, u32[]{:S(2)}) copy-start(bf16[2,256,768]{2,1,0:T(8,128)(2,1)} %param.14) | copy-start | bytes 2359300
  211.4 9.3 %copy-start.41 = (f32[512,3072]{1,0:T(8,128)S(1)}, f32[512,3072]{1,0:T(8,128)}, u32[]{:S(2)}) copy-start(f32[512,3072]{1,0:T(8,128)} %get-tuple-element.39) | copy-start | bytes 18874372
  219.1 9.3 %slice-start.4 = ((s8[4718592]{0:T(1024)(128)(4,1)}), s8[4194304]{0:T(1024)(128)(4,1)S(1)}, s32[]{:S(2)}) async-start(s8[4718592]{0:T(1024)(128)(4,1)} %bitcast.213), calls=%async_computation.31 | async-start | bytes 8388608
  220.7 7.7 %copy-start.19 = (f32[512,768]{1,0:T(8,128)}, f32[512,768]{1,0:T(8,128)S(1)}, u32[]{:S(2)}) copy-start(f32[512,768]{1,0:T(8,128)S(1)} %get-tuple-element.40) | copy-start | bytes 4718596
  220.7 7.7 %copy-start.22 = (f32[512,768]{1,0:T(8,128)S(1)}, f32[512,768]{1,0:T(8,128)}, u32[]{:S(2)}) copy-start(f32[512,768]{1,0:T(8,128)} %copy-done.21) | copy-start | bytes 4718596
  220.7 7.7 %slice-start.5 = ((s8[4718592]{0:T(1024)(128)(4,1)}), s8[524288]{0:T(1024)(128)(4,1)S(1)}, s32[]{:S(2)}) async-start(s8[4718592]{0:T(1024)(128)(4,1)} %bitcast.213), calls=%async_computation.32 | async-start | bytes 1048576
  228.5 3.1 copy-start.40
  234.9 165.3 %reduce-scatter.11.cloned.1.call-start = ((), (), s32[]{:S(2)}) async-start(), calls=%async_computation.22 | async-start | bytes 2654208 | tf_op jit(solution)/shard_map/reduce_scatter | solution.py:279
  258.0 13.3 %slice-start = ((s8[6291456]{0:T(1024)(128)(4,1)}), s8[2097152]{0:T(1024)(128)(4,1)S(1)}, s32[]{:S(2)}) async-start(s8[6291456]{0:T(1024)(128)(4,1)} %bitcast.159), calls=%async_computation.27 | async-start | bytes 4194304
  261.1 10.2 %slice-start.1 = ((s8[6291456]{0:T(1024)(128)(4,1)}), s8[4194304]{0:T(1024)(128)(4,1)S(1)}, s32[]{:S(2)}) async-start(s8[6291456]{0:T(1024)(128)(4,1)} %bitcast.159), calls=%async_computation.28 | async-start | bytes 8388608
  301.3 13.2 %slice-start.2 = ((s8[6291456]{0:T(1024)(128)(4,1)}), s8[2097152]{0:T(1024)(128)(4,1)S(1)}, s32[]{:S(2)}) async-start(s8[6291456]{0:T(1024)(128)(4,1)} %bitcast.161), calls=%async_computation.29 | async-start | bytes 4194304
  303.6 98.3 %reduce-scatter.9.cloned.1.call-start = ((), (), s32[]{:S(2)}) async-start(), calls=%async_computation.21 | async-start | bytes 2654208 | tf_op jit(solution)/shard_map/reduce_scatter | solution.py:278
  303.6 10.9 %slice-start.3 = ((s8[6291456]{0:T(1024)(128)(4,1)}), s8[4194304]{0:T(1024)(128)(4,1)S(1)}, s32[]{:S(2)}) async-start(s8[6291456]{0:T(1024)(128)(4,1)} %bitcast.161), calls=%async_computation.30 | async-start | bytes 8388608
  314.5 4.8 copy-start.4
  341.2 3.8 copy-start.15
  347.3 11.7 %copy-start.6 = (f32[2,1024,3,64]{1,3,2,0:T(8,128)S(1)}, f32[2,1024,3,64]{1,3,2,0:T(8,128)}, u32[]{:S(2)}) copy-start(f32[2,1024,3,64]{1,3,2,0:T(8,128)} %copy-done.5) | copy-start | bytes 4718596
  347.3 72.5 %reduce-scatter.7.cloned.1.call-start = ((), (), s32[]{:S(2)}) async-start(), calls=%async_computation.20 | async-start | bytes 2654208 | tf_op jit(solution)/shard_map/reduce_scatter | solution.py:277
  382.8 137.7 %reduce-scatter.15.cloned.1.call-start = ((), (), s32[]{:S(2)}) async-start(), calls=%async_computation.24 | async-start | bytes 10616832 | tf_op jit(solution)/shard_map/reduce_scatter | solution.py:281
  390.1 230.4 %reduce-scatter.17.cloned.1.call-start = ((), (), s32[]{:S(2)}) async-start(), calls=%async_computation.25 | async-start | bytes 10616832 | tf_op jit(solution)/shard_map/reduce_scatter | solution.py:282
  398.5 289.5 %all-reduce.14.cloned.1.call-start = ((), (), s32[]{:S(2)}) async-start(), calls=%async_computation.26 | async-start | bytes 3538944 | tf_op jit(solution)/shard_map/psum | solution.py:300
  421.5 240.1 %copy-start.35 = (bf16[768,768]{0,1:T(8,128)(2,1)S(1)}, bf16[768,768]{0,1:T(8,128)(2,1)}, u32[]{:S(2)}) copy-start(bf16[768,768]{0,1:T(8,128)(2,1)} %all-gather.11.cloned.1.call-done) | copy-start | bytes 3538948
  688.0 8.8 %copy-start.30 = (bf16[3072,96]{0,1:T(8,128)(2,1)S(1)}, bf16[3072,96]{0,1:T(8,128)(2,1)}, u32[]{:S(2)}) copy-start(bf16[3072,96]{0,1:T(8,128)(2,1)} %get-tuple-element.37) | copy-start | bytes 1769476
  (17 other events, 28.4 us)
Sparse Core Ops, SparseCore 0:
  9.6 25.4 all-gather.6
  36.8 22.5 all-gather.10
  61.0 22.6 all-gather.8
  85.2 22.2 all-gather.12
  108.9 51.0 all-gather.14
  161.5 49.8 all-gather.16
  235.1 35.7 reduce-scatter.12
  303.7 34.1 reduce-scatter.10
  347.5 34.1 reduce-scatter.8
  383.8 36.0 reduce-scatter.6
  422.2 98.2 reduce-scatter.14
  522.6 97.8 reduce-scatter.16
  624.9 63.0 all-reduce.13
where the time goes:
time: 711 us; the launch traced here: 705 us
  waiting for transfers between devices  316 us (44%)
  matrix products  158 us (22%)
  blocking collectives  111 us (16%)
  local copies, waits for them, and re-layouts  57.7 us (8%)
  other arithmetic  30.1 us (4%)
  between operations  16.4 us (2%)
  starting transfers between devices  16.1 us (2%)
    reduce_scatter x1, waiting for transfers between devices, shards(): lax.psum_scatter(grad_win, 'dp', scatter_dimension=1, tiled=True)  98.9 us
    reduce_scatter x1, waiting for transfers between devices, shards(): lax.psum_scatter(grad_wout, 'dp', scatter_dimension=1, tiled=True)  97.9 us
    unnamed x2, blocking collectives  42 us
    all_gather x1, waiting for transfers between devices, shards(): lax.all_gather(w_key, 'dp', axis=1, tiled=True)  24.6 us
    dot_general x6, matrix products, row_product(): lax.dot_general(left, right, (((0,), (0,)), ((), ())), preferred_element_...  23.1 us
    all_gather x1, waiting for transfers between devices, shards(): lax.all_gather(w_out, 'dp', axis=1, tiled=True)  21.4 us
    psum x1, waiting for transfers between devices, shards(): lax.psum(share_wq.astype(jnp.bfloat16), 'seq').astype(jnp.float32)  20.8 us
    dot_general x1, matrix products, shards(): pre_act = jnp.dot(hidden_low, win_full, preferred_element_type=jnp.float32)  20.7 us
  transfers between devices with their start and end apart: 17, of which 9 were waited for; matrix products, arithmetic and copies ran while one was open for 29% of the time, Pallas kernels for 0%

commit v1 on v0

--- a/solution.py
+++ b/solution.py
@@ -1,3 +1,4 @@
+import functools
 from functools import partial
 import jax
 import jax.numpy as jnp
@@ -7,6 +8,16 @@
 HEAD = 64
 highest = lax.Precision.HIGHEST
 norm_epsilon = 1e-12
+
+
+def _fix_run(s0, dim_k, array_dim):
+    return jnp.concatenate(
+        lax.all_to_all(jnp.stack(jnp.split(s0, lax.axis_size("seq"), dim_k)), "seq", 0, 0),
+        axis=array_dim,
+    )
+
+
+tell_the_object = functools.partial(_fix_run, dim_k=1, array_dim=2)
 
 
 def layer_norm(row_block, gain_vec, bias_vec):
@@ -238,12 +249,8 @@
             concat_axis=2,
             tiled=True,
         ),
-        lax.all_to_all(
-            grad_v.astype(jnp.bfloat16).reshape(seq_count, full_len, head_group * HEAD),
-            "seq",
-            split_axis=1,
-            concat_axis=2,
-            tiled=True,
+        tell_the_object(
+            grad_v.astype(jnp.bfloat16).reshape(seq_count, full_len, head_group * HEAD)
         ),
     )
     grad_q_rows = grad_q_tok.reshape(row_count, model_width)

time: 711 us -> 705 us (level)
  transfers between devices with their start and end apart: 17 -> 17, of which waited for: 9 -> 9; matrix products, arithmetic and copies ran while one was open for 29% -> 28% of each run, Pallas kernels for 0% -> 0%
where the time goes in v1:
time: 705 us; the launch traced here: 698 us
  waiting for transfers between devices  316 us (45%)
  matrix products  157 us (22%)
  blocking collectives  108 us (15%)
  local copies, waits for them, and re-layouts  53.4 us (8%)
  other arithmetic  31.6 us (4%)
  between operations  16.4 us (2%)
  starting transfers between devices  16.1 us (2%)
    reduce_scatter x1, waiting for transfers between devices, shards(): lax.psum_scatter(grad_win, 'dp', scatter_dimension=1, tiled=True)  99.1 us
    reduce_scatter x1, waiting for transfers between devices, shards(): lax.psum_scatter(grad_wout, 'dp', scatter_dimension=1, tiled=True)  97.9 us
    unnamed x2, blocking collectives  42 us
    all_gather x1, waiting for transfers between devices, shards(): lax.all_gather(w_key, 'dp', axis=1, tiled=True)  24.6 us
    dot_general x6, matrix products, row_product(): lax.dot_general(left, right, (((0,), (0,)), ((), ())), preferred_element_...  23.1 us
    all_gather x1, waiting for transfers between devices, shards(): lax.all_gather(w_out, 'dp', axis=1, tiled=True)  21.4 us
    psum x1, waiting for transfers between devices, shards(): lax.psum(share_wq.astype(jnp.bfloat16), 'seq').astype(jnp.float32)  20.8 us
    dot_general x1, matrix products, shards(): pre_act = jnp.dot(hidden_low, win_full, preferred_element_type=jnp.float32)  20.7 us
  transfers between devices with their start and end apart: 17, of which 9 were waited for; matrix products, arithmetic and copies ran while one was open for 28% of the time, Pallas kernels for 0%

profile of v1, /device:TPU:0, one launch (start us, length us, event | category | flops | bytes accessed | tf_op | source)
XLA Modules:
  0.0 698.4 jit_solution(14039726795966619966)
XLA Ops:
  10.6 24.6 %all-gather.7.cloned.1.call-done = bf16[768,768]{0,1:T(8,128)(2,1)} async-done(((bf16[768,96]{0,1:T(8,128)(2,1)}), bf16[768,768]{0,1:T(8,128)(2,1)}) %all-gather.7.cloned.1.call-update) | async-done | bytes 1179664 | tf_op jit(solution)/shard_map/all_gather | solution.py:127
  35.2 2.3 convolution_convert_fusion.3
  39.3 3.5 all-to-all-start
  43.5 15.9 %all-gather.11.cloned.1.call-done = bf16[768,768]{0,1:T(8,128)(2,1)} async-done(((bf16[768,96]{0,1:T(8,128)(2,1)}), bf16[768,768]{0,1:T(8,128)(2,1)}) %all-gather.11.cloned.1.call-update) | async-done | bytes 1179664 | tf_op jit(solution)/shard_map/all_gather | solution.py:126
  63.3 4.2 all-to-all-start.2
  69.8 16.1 %all-reduce.9 = (bf16[768]{0:T(1024)(128)(2,1)S(1)}, bf16[768]{0:T(1024)(128)(2,1)S(1)}, bf16[768]{0:T(1024)(128)(2,1)S(1)}, bf16[768]{0:T(1024)(128)(2,1)S(1)}) all-reduce(bf16[768]{0:T(1024)(128)(2,1)S(1)} %dynamic-update-slice.1, bf16[768]{0:T(1024)(128)(2,1)S(1)} %dynamic-update-slice, ...), channel_id=1, replica_groups=mesh['seq'=4,'dp'=8] {'dp'}, use_global_device_ids=true, to_apply=%add.1 | all-reduce | flops 3072 | bytes 12288
  91.9 4.4 all-to-all-start.1
  102.4 3.3 all-to-all-done.1
  108.5 2.5 reshape.222
  111.0 7.3 %fusion.20 = f32[2,1024,3,256]{1,3,2,0:T(8,128)S(1)} fusion(f32[2,1024,3,64]{1,3,2,0:T(8,128)S(1)} %reshape.236, f32[64,256]{1,0:T(8,128)S(1)} %copy-done), kind=kOutput, calls=%fused_computation.64 | convolution fusion | flops 1208352768 | bytes 7929856 | tf_op jit(solution)/shard_map/snhe,em->snhm/dot_general | solution.py:49
  118.4 7.2 %fusion.16 = (f32[2,3,256]{2,1,0:T(4,128)S(1)}, f32[2,1024,3,256]{3,1,2,0:T(8,128)S(1)}) fusion(f32[2,1024]{1,0:T(2,128)S(1)} %compare_convert_fusion, f32[2,1024,3]{1,2,0:T(4,128)S(1)} %broadcast_multiply_fusion.3, f32[64,256]{1,0:T(8,128)S(1)} %copy-done, f32[2,1024,3,64]{1,3,2,0:T(8,128)S(1)} %reshape.235), kind=kOutput, calls=%fused_computation.31 | convolution fusion | flops 1213069824 | bytes 7968768 | tf_op jit(solution)/shard_map/snhe,em->snhm/dot_general | solution.py:49
  125.6 3.6 fusion.9
  129.3 3.6 fusion.17
  132.9 5.6 fusion.53
  140.4 3.5 all-to-all-start.3
  144.6 12.5 %all-to-all-done.3 = bf16[2,1024,192]{2,0,1:T(2,128)(2,1)S(1)} async-done(((bf16[2,1024,192]{2,0,1:T(2,128)(2,1)}), bf16[2,1024,192]{2,0,1:T(2,128)(2,1)S(1)}, u32[]{:S(2)}, u32[]{:S(2)}) %all-to-all-start.3) | async-done | bytes 786464 | tf_op jit(solution)/shard_map/all_to_all | solution.py:177
  158.1 4.2 copy.105
  165.3 2.5 fusion.54
  169.2 20.7 %multiply_convert_fusion = (bf16[512,3072]{1,0:T(8,128)(2,1)}, f32[512,3072]{1,0:T(8,128)}, f32[512,3072]{1,0:T(8,128)}) fusion(bf16[768,3072]{1,0:T(8,128)(2,1)} %all-gather.15.cloned.1.call-done, f32[512,768]{1,0:T(8,128)} %copy-done.21, f32[768]{0:T(1024)S(1)} %convert_element_type.205, f32[768]{0:T(1024)S(1)} %convert_element_type.204, ...), kind=kOutput, calls=%fused_computation.6 | convolution fusion | flops 2520121344 | bytes 22030336 | tf_op jit(solution)/shard_map/dot_general | solution.py:183
  190.0 21.4 %all-gather.17.cloned.1.call-done = bf16[3072,768]{0,1:T(8,128)(2,1)} async-done(((bf16[3072,96]{0,1:T(8,128)(2,1)}), bf16[3072,768]{0,1:T(8,128)(2,1)}) %all-gather.17.cloned.1.call-update) | async-done | bytes 4718608 | tf_op jit(solution)/shard_map/all_gather | solution.py:131
  211.4 6.6 fusion.55
  220.7 7.7 %add_convert_fusion = bf16[512,3072]{1,0:T(8,128)(2,1)S(1)} fusion(f32[512,3072]{1,0:T(8,128)S(1)} %copy-done.41, f32[512,3072]{1,0:T(8,128)} %get-tuple-element.56, bf16[3072,768]{0,1:T(8,128)(2,1)S(1)} %copy-done.33, f32[512,768]{1,0:T(8,128)S(1)} %get-tuple-element.40), kind=kOutput, calls=%fused_computation.5 | convolution fusion | flops 2438332416 | bytes 22020096 | tf_op jit(solution)/shard_map/dot_general | solution.py:210
  228.5 3.1 multiply_reduce_fusion.1
  232.7 2.3 fusion.28
  235.0 2.9 convolution_convert_fusion
  238.0 2.3 copy.80
  240.3 15.4 %all_to_all.92 = bf16[2,256,768]{1,0,2:T(2,128)(2,1)S(1)} all-to-all(bf16[2,256,768]{1,0,2:T(2,128)(2,1)S(1)} %copy.80), channel_id=1, replica_groups=mesh['seq'=4,'dp'=8] {'seq'}, dimensions={2} | all-to-all | bytes 1572864 | tf_op jit(solution)/shard_map/all_to_all | solution.py:226
  258.1 3.1 reshape.239
  261.1 10.2 %fusion.8 = f32[2,3,256,64]{2,3,1,0:T(8,128)S(1)} fusion(f32[2,1024,3,256]{1,3,2,0:T(8,128)} %copy-done.1, f32[2,1024,3]{1,2,0:T(4,128)S(1)} %broadcast_multiply_fusion.2, f32[2,1024,3,64]{1,3,2,0:T(8,128)} %reshape.239, f32[2,1024,3]{1,2,0:T(4,128)S(1)} %bitcast.218), kind=kOutput, calls=%fused_computation.23 | convolution fusion | flops 1209925632 | bytes 8306688 | tf_op jit(solution)/shard_map/snhm,snhe->shme/dot_general | solution.py:91
  271.4 7.2 %fusion.24 = bf16[2,3,64,1024]{3,2,1,0:T(8,128)(2,1)S(1)} fusion(f32[2,3,256,64]{2,3,1,0:T(8,128)S(1)} %fusion.8, f32[2,1024,3,256]{3,1,2,0:T(8,128)S(1)} %bitcast.171, f32[2,1024]{1,0:T(2,128)S(1)} %compare_convert_fusion, f32[2,1024,3]{1,2,0:T(4,128)S(1)} %broadcast_multiply_fusion.3), kind=kOutput, calls=%fused_computation.74 | convolution fusion | flops 1211498496 | bytes 7503872 | tf_op jit(solution)/shard_map/snhm,shme->snhe/dot_general | solution.py:99
  281.0 13.0 %all_to_all.93 = bf16[4,2,256,192]{2,1,3,0:T(2,128)(2,1)S(1)} all-to-all(bf16[4,2,256,192]{2,1,3,0:T(2,128)(2,1)S(1)} %pad_maximum_fusion), channel_id=1, replica_groups=mesh['seq'=4,'dp'=8] {'seq'}, dimensions={0} | all-to-all | bytes 1572864 | tf_op jit(solution)/shard_map/all_to_all | solution.py:15
  297.4 2.4 multiply_reduce_fusion.2
  299.8 8.4 %fusion.7 = f32[2,3,1,256]{3,2,1,0:T(1,128)S(1)} fusion(f32[2,1024,3,256]{1,3,2,0:T(8,128)} %copy-done.1, f32[2,1024,3]{1,2,0:T(4,128)S(1)} %broadcast_multiply_fusion.2, f32[2,1024,3,1]{1,2,0,3:T(4,128)S(1)} %bitcast.220), kind=kOutput, calls=%fused_computation.22 | convolution fusion | flops 20447232 | bytes 6346752 | tf_op jit(solution)/shard_map/snhm,snh->shm/dot_general | solution.py:92
  308.3 4.8 fusion.56
  313.1 6.2 multiply_convert_fusion.1
  320.2 14.7 %all_to_all.94 = bf16[2,1024,192]{2,0,1:T(2,128)(2,1)S(1)} all-to-all(bf16[2,1024,192]{2,0,1:T(2,128)(2,1)S(1)} %copy.89), channel_id=1, replica_groups=mesh['seq'=4,'dp'=8] {'seq'}, dimensions={1} | all-to-all | bytes 1572864 | tf_op jit(solution)/shard_map/all_to_all | solution.py:245
  338.8 2.3 convolution_bitcast_fusion.1
  341.2 11.6 %fusion.57 = (f32[2,1024,3]{1,2,0:T(4,128)S(1)}, f32[2,1024,3,256]{1,3,2,0:T(8,128)S(1)}) fusion(f32[2,1024,3,256]{1,3,2,0:T(8,128)} %copy-done.1, f32[2,1024,3]{1,2,0:T(4,128)S(1)} %broadcast_multiply_fusion.2, f32[2,3,256]{2,1,0:T(4,128)S(1)} %get-tuple-element.50, f32[2,1024,3]{1,2,0:T(4,128)S(1)} %negate_divide_fusion, ...), kind=kOutput, calls=%fused_computation.131 | convolution fusion | flops 1216210944 | bytes 14653440 | tf_op jit(solution)/shard_map/snhe,shme->snhm/dot_general | solution.py:88
  352.8 4.3 multiply_convert_fusion.2
  358.0 13.4 %all_to_all.95 = bf16[2,1024,192]{2,0,1:T(2,128)(2,1)S(1)} all-to-all(bf16[2,1024,192]{2,0,1:T(2,128)(2,1)S(1)} %copy.84), channel_id=1, replica_groups=mesh['seq'=4,'dp'=8] {'seq'}, dimensions={1} | all-to-all | bytes 1572864 | tf_op jit(solution)/shard_map/all_to_all | solution.py:238
  376.6 7.2 %fusion.46 = f32[768,3072]{1,0:T(8,128)} fusion(bf16[512,3072]{1,0:T(8,128)(2,1)} %copy-done.40, f32[512,768]{1,0:T(8,128)S(1)} %copy-done.23, f32[768]{0:T(1024)S(1)} %convert_element_type.205, f32[768]{0:T(1024)S(1)} %convert_element_type.204, f32[512]{0:T(512)S(1)} %add_rsqrt_fusion.1, f32[512]{0:T(512)S(1)} %broadcast_multiply_fusion.8), kind=kOutput, calls=%fused_computation.123 | convolution fusion | flops 2417885184 | bytes 14166016 | tf_op jit(solution)/shard_map/dot_general | solution.py:42
  385.2 7.0 %fusion.31 = f32[3072,768]{0,1:T(8,128)} fusion(bf16[512,3072]{1,0:T(8,128)(2,1)} %get-tuple-element.38, f32[512,768]{1,0:T(8,128)S(1)} %copy-done.20), kind=kOutput, calls=%fused_computation.84 | convolution fusion | flops 2416312320 | bytes 14155776 | tf_op jit(solution)/shard_map/dot_general | solution.py:42
  397.2 16.3 %reduce-scatter.7.cloned.1.call-done = f32[768,96]{0,1:T(8,128)} async-done(((f32[768,768]{0,1:T(8,128)}), f32[768,96]{0,1:T(8,128)}) %reduce-scatter.7.cloned.1.call-update) | async-done | bytes 294928 | tf_op jit(solution)/shard_map/reduce_scatter | solution.py:284
  415.1 99.1 %reduce-scatter.15.cloned.1.call-done = f32[768,384]{1,0:T(8,128)} async-done(((f32[768,3072]{1,0:T(8,128)}), f32[768,384]{1,0:T(8,128)}) %reduce-scatter.15.cloned.1.call-update) | async-done | bytes 1179664 | tf_op jit(solution)/shard_map/reduce_scatter | solution.py:288
  516.4 97.9 %reduce-scatter.17.cloned.1.call-done = f32[3072,96]{0,1:T(8,128)} async-done(((f32[3072,768]{0,1:T(8,128)}), f32[3072,96]{0,1:T(8,128)}) %reduce-scatter.17.cloned.1.call-update) | async-done | bytes 1179664 | tf_op jit(solution)/shard_map/reduce_scatter | solution.py:289
  617.1 25.9 %all-reduce.8 = (bf16[768]{0:T(1024)(128)(2,1)S(1)}, bf16[768]{0:T(1024)(128)(2,1)S(1)}, bf16[768]{0:T(1024)(128)(2,1)S(1)}, bf16[768]{0:T(1024)(128)(2,1)S(1)}) all-reduce(f32[768]{0:T(1024)S(1)} %get-tuple-element.12, f32[768]{0:T(1024)S(1)} %get-tuple-element.17, ...), channel_id=8, replica_groups=mesh['seq'=4,'dp'=8] {'dp'}, use_global_device_ids=true, to_apply=%region_27.0.clone | all-reduce | flops 3072 | bytes 18432
  643.4 9.9 %all-reduce.10 = (bf16[96]{0:T(256)(128)(2,1)S(1)}, bf16[96]{0:T(256)(128)(2,1)S(1)}, bf16[96]{0:T(256)(128)(2,1)S(1)}, bf16[96]{0:T(256)(128)(2,1)S(1)}) all-reduce(bf16[96]{0:T(256)(128)(2,1)S(1)} %dynamic-slice.19, bf16[96]{0:T(256)(128)(2,1)S(1)} %dynamic-slice.18, ...), channel_id=1, replica_groups=mesh['seq'=4,'dp'=8] {'seq'}, use_global_device_ids=true, to_apply=%region_28.0 | all-reduce | flops 384 | bytes 1536 | tf_op jit(solution)/shard_map/psum | solution.py:313
  661.0 20.8 %all-reduce.14.cloned.1.call-done = (bf16[768,96]{0,1:T(8,128)(2,1)}, bf16[768,96]{0,1:T(8,128)(2,1)}, bf16[768,96]{0,1:T(8,128)(2,1)}, bf16[768,96]{0,1:T(8,128...) async-done(((bf16[768,96]{0,1:T(8,128)(2,1)}, bf16[768,96]{0,1:T(8,128)(2,1)}, bf16[768,96]{0,1:T(8,128)(2,1)}, bf16[768,96]{0,1:T(8,128)(2,1)}, ...) | async-done | bytes 1769488 | tf_op jit(solution)/shard_map/psum | solution.py:307
  (234 shorter events, 87.0 us)
Async XLA Ops:
  7.2 103.8 %copy-start = (f32[64,256]{1,0:T(8,128)S(1)}, f32[64,256]{1,0:T(8,128)}, u32[]{:S(2)}) copy-start(f32[64,256]{1,0:T(8,128)} %param.16) | copy-start | bytes 196612
  7.2 28.0 %all-gather.7.cloned.1.call-start = ((), (), s32[]{:S(2)}) async-start(), calls=%async_computation.14 | async-start | bytes 1327104 | tf_op jit(solution)/shard_map/all_gather | solution.py:127
  7.9 51.4 %all-gather.11.cloned.1.call-start = ((), (), s32[]{:S(2)}) async-start(), calls=%async_computation.16 | async-start | bytes 1327104 | tf_op jit(solution)/shard_map/all_gather | solution.py:126
  8.7 77.2 %all-gather.9.cloned.1.call-start = ((), (), s32[]{:S(2)}) async-start(), calls=%async_computation.15 | async-start | bytes 1327104 | tf_op jit(solution)/shard_map/all_gather | solution.py:128
  9.4 155.8 %all-gather.13.cloned.1.call-start = ((), (), s32[]{:S(2)}) async-start(), calls=%async_computation.17 | async-start | bytes 1327104 | tf_op jit(solution)/shard_map/all_gather | solution.py:129
  10.0 159.2 %all-gather.15.cloned.1.call-start = ((), (), s32[]{:S(2)}) async-start(), calls=%async_computation.18 | async-start | bytes 5308416 | tf_op jit(solution)/shard_map/all_gather | solution.py:130
  37.5 5.9 copy-start.32
  37.5 21.9 %copy-start.12 = (bf16[2,256,768]{2,1,0:T(8,128)(2,1)S(1)}, bf16[2,256,768]{2,1,0:T(8,128)(2,1)}, u32[]{:S(2)}) copy-start(bf16[2,256,768]{2,1,0:T(8,128)(2,1)} %param.14) | copy-start | bytes 2359300
  39.3 24.0 %all-to-all-start = ((bf16[2,256,768]{1,0,2:T(2,128)(2,1)}), bf16[2,256,768]{1,0,2:T(2,128)(2,1)S(1)}, u32[]{:S(2)}, u32[]{:S(2)}) async-start(bf16[2,256,768]{1,0,2:T(2,128)(2,1)} %copy.67), calls=%async_computation | async-start | bytes 1572864 | tf_op jit(solution)/shard_map/all_to_all | solution.py:153
  42.9 168.6 %all-gather.17.cloned.1.call-start = ((), (), s32[]{:S(2)}) async-start(), calls=%async_computation.19 | async-start | bytes 5308416 | tf_op jit(solution)/shard_map/all_gather | solution.py:131
  61.5 6.1 copy-start.31
  61.5 7.4 %copy-start.36 = (bf16[96]{0:T(256)(128)(2,1)S(1)}, bf16[96]{0:T(256)(128)(2,1)}, u32[]{:S(2)}) copy-start(bf16[96]{0:T(256)(128)(2,1)} %param.26) | copy-start | bytes 580
  61.5 7.6 %copy-start.37 = (bf16[96]{0:T(256)(128)(2,1)S(1)}, bf16[96]{0:T(256)(128)(2,1)}, u32[]{:S(2)}) copy-start(bf16[96]{0:T(256)(128)(2,1)} %param.23) | copy-start | bytes 580
  61.5 7.8 %copy-start.38 = (bf16[96]{0:T(256)(128)(2,1)S(1)}, bf16[96]{0:T(256)(128)(2,1)}, u32[]{:S(2)}) copy-start(bf16[96]{0:T(256)(128)(2,1)} %param.24) | copy-start | bytes 580
  61.5 8.0 %copy-start.39 = (bf16[96]{0:T(256)(128)(2,1)S(1)}, bf16[96]{0:T(256)(128)(2,1)}, u32[]{:S(2)}) copy-start(bf16[96]{0:T(256)(128)(2,1)} %param.25) | copy-start | bytes 580
  63.3 28.6 %all-to-all-start.2 = ((bf16[2,256,768]{1,0,2:T(2,128)(2,1)}), bf16[2,256,768]{1,0,2:T(2,128)(2,1)}, u32[]{:S(2)}, u32[]{:S(2)}) async-start(bf16[2,256,768]{1,0,2:T(2,128)(2,1)} %copy.73), calls=%async_computation.2 | async-start | bytes 1572864 | tf_op jit(solution)/shard_map/all_to_all | solution.py:146
  91.9 26.5 %copy-start.3 = (f32[2,1024,3,64]{1,3,2,0:T(8,128)}, f32[2,1024,3,64]{1,3,2,0:T(8,128)S(1)}, u32[]{:S(2)}) copy-start(f32[2,1024,3,64]{1,3,2,0:T(8,128)S(1)} %reshape.235) | copy-start | bytes 4718596
  91.9 13.8 %all-to-all-start.1 = ((bf16[2,256,768]{1,0,2:T(2,128)(2,1)}), bf16[2,256,768]{1,0,2:T(2,128)(2,1)}, u32[]{:S(2)}, u32[]{:S(2)}) async-start(bf16[2,256,768]{1,0,2:T(2,128)(2,1)} %copy.70), calls=%async_computation.1 | async-start | bytes 1572864 | tf_op jit(solution)/shard_map/all_to_all | solution.py:160
  101.9 9.1 %copy-start.5 = (f32[2,1024,3,64]{1,3,2,0:T(8,128)}, f32[2,1024,3,64]{1,3,2,0:T(8,128)S(1)}, u32[]{:S(2)}) copy-start(f32[2,1024,3,64]{1,3,2,0:T(8,128)S(1)} %reshape.236) | copy-start | bytes 4718596
  118.4 14.5 %copy-start.1 = (f32[2,1024,3,256]{1,3,2,0:T(8,128)}, f32[2,1024,3,256]{1,3,2,0:T(8,128)S(1)}, u32[]{:S(2)}) copy-start(f32[2,1024,3,256]{1,3,2,0:T(8,128)S(1)} %fusion.20) | copy-start | bytes 18874372
  125.6 3.7 copy-start.2
  125.6 3.7 copy-start.10
  132.8 5.6 copy-start.25
  138.4 5.7 copy-start.11
  140.4 16.7 %all-to-all-start.3 = ((bf16[2,1024,192]{2,0,1:T(2,128)(2,1)}), bf16[2,1024,192]{2,0,1:T(2,128)(2,1)S(1)}, u32[]{:S(2)}, u32[]{:S(2)}) async-start(bf16[2,1024,192]{2,0,1:T(2,128)(2,1)} %copy.77), calls=%async_computation.3 | async-start | bytes 2097152 | tf_op jit(solution)/shard_map/all_to_all | solution.py:177
  144.0 248.3 %reduce-scatter.13.cloned.1.call-start = ((), (), s32[]{:S(2)}) async-start(), calls=%async_computation.23 | async-start | bytes 2654208 | tf_op jit(solution)/shard_map/reduce_scatter | solution.py:287
  158.1 7.2 %copy-start.13 = (bf16[2,256,768]{2,1,0:T(8,128)(2,1)S(1)}, bf16[2,256,768]{2,1,0:T(8,128)(2,1)}, u32[]{:S(2)}) copy-start(bf16[2,256,768]{2,1,0:T(8,128)(2,1)} %param.14) | copy-start | bytes 2359300
  211.4 9.3 %copy-start.41 = (f32[512,3072]{1,0:T(8,128)S(1)}, f32[512,3072]{1,0:T(8,128)}, u32[]{:S(2)}) copy-start(f32[512,3072]{1,0:T(8,128)} %get-tuple-element.39) | copy-start | bytes 18874372
  219.1 9.3 %slice-start.4 = ((s8[4718592]{0:T(1024)(128)(4,1)}), s8[4194304]{0:T(1024)(128)(4,1)S(1)}, s32[]{:S(2)}) async-start(s8[4718592]{0:T(1024)(128)(4,1)} %bitcast.226), calls=%async_computation.31 | async-start | bytes 8388608
  220.7 7.7 %copy-start.19 = (f32[512,768]{1,0:T(8,128)}, f32[512,768]{1,0:T(8,128)S(1)}, u32[]{:S(2)}) copy-start(f32[512,768]{1,0:T(8,128)S(1)} %get-tuple-element.40) | copy-start | bytes 4718596
  220.7 7.7 %copy-start.22 = (f32[512,768]{1,0:T(8,128)S(1)}, f32[512,768]{1,0:T(8,128)}, u32[]{:S(2)}) copy-start(f32[512,768]{1,0:T(8,128)} %copy-done.21) | copy-start | bytes 4718596
  220.7 7.7 %slice-start.5 = ((s8[4718592]{0:T(1024)(128)(4,1)}), s8[524288]{0:T(1024)(128)(4,1)S(1)}, s32[]{:S(2)}) async-start(s8[4718592]{0:T(1024)(128)(4,1)} %bitcast.226), calls=%async_computation.32 | async-start | bytes 1048576
  235.0 159.0 %reduce-scatter.11.cloned.1.call-start = ((), (), s32[]{:S(2)}) async-start(), calls=%async_computation.22 | async-start | bytes 2654208 | tf_op jit(solution)/shard_map/reduce_scatter | solution.py:286
  258.1 13.3 %slice-start = ((s8[6291456]{0:T(1024)(128)(4,1)}), s8[2097152]{0:T(1024)(128)(4,1)S(1)}, s32[]{:S(2)}) async-start(s8[6291456]{0:T(1024)(128)(4,1)} %bitcast.170), calls=%async_computation.27 | async-start | bytes 4194304
  261.1 10.2 %slice-start.1 = ((s8[6291456]{0:T(1024)(128)(4,1)}), s8[4194304]{0:T(1024)(128)(4,1)S(1)}, s32[]{:S(2)}) async-start(s8[6291456]{0:T(1024)(128)(4,1)} %bitcast.170), calls=%async_computation.28 | async-start | bytes 8388608
  279.5 15.6 %copy-start.14 = (bf16[2,256,768]{2,1,0:T(8,128)(2,1)S(1)}, bf16[2,256,768]{2,1,0:T(8,128)(2,1)}, u32[]{:S(2)}) copy-start(bf16[2,256,768]{2,1,0:T(8,128)(2,1)} %param.14) | copy-start | bytes 2359300
  295.1 13.2 %slice-start.2 = ((s8[6291456]{0:T(1024)(128)(4,1)}), s8[2097152]{0:T(1024)(128)(4,1)S(1)}, s32[]{:S(2)}) async-start(s8[6291456]{0:T(1024)(128)(4,1)} %bitcast.172), calls=%async_computation.29 | async-start | bytes 4194304
  297.3 98.3 %reduce-scatter.9.cloned.1.call-start = ((), (), s32[]{:S(2)}) async-start(), calls=%async_computation.21 | async-start | bytes 2654208 | tf_op jit(solution)/shard_map/reduce_scatter | solution.py:285
  297.4 10.9 %slice-start.3 = ((s8[6291456]{0:T(1024)(128)(4,1)}), s8[4194304]{0:T(1024)(128)(4,1)S(1)}, s32[]{:S(2)}) async-start(s8[6291456]{0:T(1024)(128)(4,1)} %bitcast.172), calls=%async_computation.30 | async-start | bytes 8388608
  308.2 4.8 copy-start.4
  335.0 3.8 copy-start.15
  341.1 11.7 %copy-start.6 = (f32[2,1024,3,64]{1,3,2,0:T(8,128)S(1)}, f32[2,1024,3,64]{1,3,2,0:T(8,128)}, u32[]{:S(2)}) copy-start(f32[2,1024,3,64]{1,3,2,0:T(8,128)} %copy-done.5) | copy-start | bytes 4718596
  341.1 72.4 %reduce-scatter.7.cloned.1.call-start = ((), (), s32[]{:S(2)}) async-start(), calls=%async_computation.20 | async-start | bytes 2654208 | tf_op jit(solution)/shard_map/reduce_scatter | solution.py:284
  376.5 137.7 %reduce-scatter.15.cloned.1.call-start = ((), (), s32[]{:S(2)}) async-start(), calls=%async_computation.24 | async-start | bytes 10616832 | tf_op jit(solution)/shard_map/reduce_scatter | solution.py:288
  383.9 230.4 %reduce-scatter.17.cloned.1.call-start = ((), (), s32[]{:S(2)}) async-start(), calls=%async_computation.25 | async-start | bytes 10616832 | tf_op jit(solution)/shard_map/reduce_scatter | solution.py:289
  392.2 289.5 %all-reduce.14.cloned.1.call-start = ((), (), s32[]{:S(2)}) async-start(), calls=%async_computation.26 | async-start | bytes 3538944 | tf_op jit(solution)/shard_map/psum | solution.py:307
  415.1 240.2 %copy-start.35 = (bf16[768,768]{0,1:T(8,128)(2,1)S(1)}, bf16[768,768]{0,1:T(8,128)(2,1)}, u32[]{:S(2)}) copy-start(bf16[768,768]{0,1:T(8,128)(2,1)} %all-gather.11.cloned.1.call-done) | copy-start | bytes 3538948
  681.8 8.8 %copy-start.30 = (bf16[3072,96]{0,1:T(8,128)(2,1)S(1)}, bf16[3072,96]{0,1:T(8,128)(2,1)}, u32[]{:S(2)}) copy-start(bf16[3072,96]{0,1:T(8,128)(2,1)} %get-tuple-element.37) | copy-start | bytes 1769476
  (17 other events, 29.6 us)
Sparse Core Ops, SparseCore 0:
  9.6 25.4 all-gather.6
  36.8 22.5 all-gather.10
  61.0 22.5 all-gather.8
  85.1 22.3 all-gather.12
  108.9 51.0 all-gather.14
  161.5 49.8 all-gather.16
  235.1 35.8 reduce-scatter.12
  297.4 34.2 reduce-scatter.10
  341.2 34.1 reduce-scatter.8
  377.6 35.9 reduce-scatter.6
  415.8 98.3 reduce-scatter.14
  516.4 97.8 reduce-scatter.16
  618.7 63.0 all-reduce.13
